TPU v7x, 32 devices: a whole 2x2x4 slice. The times are simulated.
32 devices in a mesh: blk: 8 (over y, x, core), space: 4 (over z).
Axes of the slice: x: 2, y: 2, z: 4, core: 2. Of those that a mesh axis runs over, the one named last changes fastest.
Arguments:
- electrons: bfloat16 [8, 8, 2, 64, 4096], P('blk', None, None, 'space'), may hold values from -4 to 4
- holes: bfloat16 [8, 8, 2, 64, 4096], P('blk', None, None, 'space'), may hold values from -4 to 4
- pair_order: int32 [8, 2], P('blk'), may hold values from 0 to 1, each once within a row
Outputs:
- potential: float32 [8, 2, 64, 64, 128], P('blk', None, 'space')
- coulomb: float32 [8, 2, 2, 2], P('blk')
Inputs may be any that keep to these rules, and one draw needn't show every extreme that they name: `pair_order`: each row lists every candidate once.
All inputs are finite; a program needn't handle non-finite values.
Results may differ from a plain program's by a relative error of at most 0.0003.
Values may be sent and summed in bfloat16 or wider, within the bound.
A program may use at most 64 MiB of HBM per device.

v0:
```python
from functools import partial
import math
import jax
import jax.numpy as jnp
from jax import lax
from jax.sharding import PartitionSpec as P

NX = 64
NY = 64
NZ = 64
SCREENING = 0.01
PRECISE = lax.Precision.HIGHEST


def shifted(block, axis, distance):
    devices = range(lax.axis_size(axis))
    route = [((i - distance) % len(devices), i) for i in devices]
    return lax.ppermute(block, axis, route)


def phase_tables(points, direction):
    positions = jnp.arange(points, dtype=jnp.int32)
    products = positions[:, None] * positions[None, :] % points
    angles = 2.0 * math.pi / points * products.astype(jnp.float32)
    return (jnp.cos(angles), direction * jnp.sin(angles))


def depth_matrix(points, direction):
    cosines, sines = phase_tables(points, direction)
    upper = jnp.concatenate([cosines, -sines], axis=1)
    lower = jnp.concatenate([sines, cosines], axis=1)
    return jnp.concatenate([upper, lower], axis=0)


def turned(values):
    middle = values.shape[-1] // 2
    return jnp.concatenate([values[..., middle:], -values[..., :middle]], axis=-1)


def along_rows(values, direction):
    cosines, sines = phase_tables(values.shape[1], direction)
    tables = jnp.stack([cosines, sines])
    stacked = jnp.stack([values, turned(values)])
    return jnp.einsum("tkn,tpnbc->pkbc", tables, stacked, precision=PRECISE)


def along_columns(values, direction):
    cosines, sines = phase_tables(values.shape[2], direction)
    tables = jnp.stack([cosines, sines])
    stacked = jnp.stack([values, turned(values)])
    return jnp.einsum("tkn,tpanc->pakc", tables, stacked, precision=PRECISE)


def along_depth(values, direction):
    matrix = depth_matrix(values.shape[-1] // 2, direction)
    return jnp.einsum("pabn,nk->pabk", values, matrix, precision=PRECISE)


def lattice_term(indices, points):
    return 2.0 - 2.0 * jnp.cos(2.0 * math.pi / points * (indices % points).astype(jnp.float32))


def green_block(start_y, rows_y):
    index_x = jnp.arange(NX, dtype=jnp.int32)
    index_y = start_y + jnp.arange(rows_y, dtype=jnp.int32)
    index_z = jnp.arange(2 * NZ, dtype=jnp.int32)
    term_x = lattice_term(index_x, NX)
    term_y = lattice_term(index_y, NY)
    term_z = lattice_term(index_z, NZ)
    green = 1.0 / (
        term_x[:, None, None] + term_y[None, :, None] + term_z[None, None, :] + SCREENING
    )
    anchor = (
        (index_x[:, None, None] == 0)
        & (index_y[None, :, None] == 0)
        & (index_z[None, None, :] % NZ == 0)
    )
    return jnp.where(anchor, jnp.zeros_like(green), green)


def pair_densities(electrons, hole_set):

    def banded(first_set, second_set):
        return jnp.einsum(
            "ebxc,hbxc->hexc", first_set, second_set, preferred_element_type=jnp.float32
        )

    real_part = banded(electrons[:, :, 0], hole_set[:, :, 0]) + banded(
        electrons[:, :, 1], hole_set[:, :, 1]
    )
    imag_part = banded(electrons[:, :, 0], hole_set[:, :, 1]) - banded(
        electrons[:, :, 1], hole_set[:, :, 0]
    )
    target_shape = (real_part.shape[0] * real_part.shape[1], real_part.shape[2], NY, NZ)
    return jnp.concatenate(
        [real_part.reshape(target_shape), imag_part.reshape(target_shape)], axis=-1
    )


def fetch_previous(holes):
    return shifted(holes, "blk", 1)


def plane_spectra(densities):
    return along_columns(along_depth(densities, 1.0), 1.0)


def column_spectra(block, start_y):
    spectra = along_rows(block, 1.0)
    return (spectra, spectra * green_block(start_y, block.shape[2])[None])


def finish_inverse(block, factor):
    return along_depth(along_columns(block, -1.0), -1.0) * factor


def inverse_field(weighted, factor):
    return finish_inverse(
        lax.all_to_all(
            along_rows(weighted, -1.0), "space", split_axis=1, concat_axis=2, tiled=True
        ),
        factor=factor,
    )


def pair_products(first_set, second_set):
    flat_first = first_set.reshape(first_set.shape[0], -1)
    stacked = jnp.stack([second_set, -turned(second_set)]).reshape(2, second_set.shape[0], -1)
    return jnp.einsum("pn,tqn->tpq", flat_first, stacked, precision=PRECISE)


def shards(electrons, holes, pair_order):
    rows_y = NY // lax.axis_size("space")
    start_y = lax.axis_index("space") * rows_y
    factor = 1.0 / (NX * NY * NZ)
    forward = partial(column_spectra, start_y=start_y)
    previous = fetch_previous(holes)
    densities = pair_densities(electrons, jnp.concatenate([holes, previous], axis=0))
    spectra, weighted = forward(
        lax.all_to_all(plane_spectra(densities), "space", split_axis=2, concat_axis=1, tiled=True)
    )
    partial_sums = pair_products(weighted, spectra) * (factor * factor)
    potential_field = inverse_field(weighted, factor)
    totals = lax.psum(partial_sums, "space")
    pair_rank = pair_order[0]
    coulomb = jnp.take(jnp.take(totals, pair_rank, axis=1), pair_rank, axis=2)
    potential = jnp.take(potential_field, pair_rank, axis=0)
    return (potential[None], coulomb[None])


def solution(mesh):
    in_specs = (
        P("blk", None, None, "space", None),
        P("blk", None, None, "space", None),
        P("blk", None),
    )
    out_specs = (P("blk", None, "space", None, None), P("blk", None, None, None))
    return jax.shard_map(shards, mesh=mesh, in_specs=in_specs, out_specs=out_specs, check_vma=False)
```

profile of v0, /device:TPU:0, one launch (start us, length us, event | category | flops | bytes accessed | tf_op | source)
XLA Modules:
  0.0 122.4 jit_solution(10038824163050638869)
XLA Ops:
  0.6 0.5 collective-permute-start
  1.2 0.1 fusion.82
  1.3 0.1 fusion.71
  1.4 0.1 fusion.69
  1.6 0.1 fusion.67
  1.7 0.0 copy-start
  1.7 1.9 %constant_dynamic-update-slice_fusion.1 = bf16[2,8,2,16,4096]{4,3,2,1,0:T(8,128)(2,1)S(1)} fusion(bf16[1,8,2,16,4096]{4,3,2,1,0:T(8,128)(2,1)} %param.4), kind=kLoop, calls=%fused_computation.107 | loop fusion | bytes 4194304
  3.6 0.3 copy-done
  3.9 0.5 bitcast_convert_fusion.1
  4.4 23.6 %collective-permute-done = bf16[1,8,2,16,4096]{4,3,2,1,0:T(8,128)(2,1)S(1)} collective-permute-done((bf16[1,8,2,16,4096]{4,3,2,1,0:T(8,128)(2,1)}, bf16[1,8,2,16,4096]{4,3,2,1,0:T(8,128)(2,1)S(1)}, u32[]{:S(2)}, u32[]{:S(2)}) %collective-permute-start) | collective-permute-done | bytes 2097184 | tf_op jit(solution)/shard_map/ppermute | solution.py:18
  28.0 0.2 constant_dynamic-update-slice_fusion
  28.2 1.7 %fusion.2 = (f32[16,4096,2]{1,0,2:T(8,128)S(1)}, f32[16,4096,2]{1,0,2:T(8,128)S(1)}, f32[16,4096,2]{1,0,2:T(8,128)S(1)}, f32[16,4096,2]{1,0,2:T(8,128)S(1)}) fusion(f32[16,4096,8]{1,0,2:T(8,128)S(1)} %get-tuple-element.9, bf16[2,8,2,16,4096]{4,3,2,1,0:T(8,128)(2,1)S(1)} %constant_dynamic-update-slice_fusion, f32[16,4096,8]{1,0,2:T(8,128)S(1)} %get-tuple-element.8), kind=kLoop, calls=%fused_computation.9 | loop fusion | flops 9961472 | bytes 10485760 | tf_op jit(solution)/shard_map/ebxc,hbxc->hexc/dot_general | solution.py:84
  29.9 0.1 subtract_bitcast_fusion
  30.0 0.4 reshape.326
  30.4 0.4 reshape.325
  30.8 1.1 fusion.32
  31.9 0.4 fusion.95
  32.3 0.3 maximum_bitcast_fusion
  32.7 1.3 %fusion.16 = f32[2,16,64,128]{3,2,0,1:T(8,128)S(1)} fusion(f32[1,64,64]{2,1,0:T(8,128)S(1)} %get-tuple-element.27, f32[1,64,64]{2,1,0:T(8,128)S(1)} %get-tuple-element.26, f32[1,2,16,64,128]{4,3,2,1,0:T(8,128)S(1)} %maximum_bitcast_fusion, f32[1,2,16,64,128]{4,3,2,1,0:T(8,128)S(1)} %bitcast.148), kind=kOutput, calls=%fused_computation.29 | convolution fusion | flops 403185664 | bytes 3178496 | tf_op jit(solution)/shard_map/tkn,tpanc->pakc/dot_general | solution.py:51
  34.0 0.0 copy-start.2
  34.0 1.6 %copy.36 = f32[2,16,64,128]{3,1,0,2:T(8,128)} copy(f32[2,16,64,128]{3,2,0,1:T(8,128)S(1)} %fusion.16) | data formatting | bytes 2097152 | tf_op jit(solution)/shard_map/tkn,tpanc->pakc/transpose | solution.py:51
  35.6 5.6 %all-to-all-start = ((f32[2,16,64,128]{3,1,0,2:T(8,128)}), f32[2,16,64,128]{3,1,0,2:T(8,128)S(1)}, u32[]{:S(2)}, u32[]{:S(2)}) async-start(f32[2,16,64,128]{3,1,0,2:T(8,128)} %copy.36), calls=%async_computation | async-start | bytes 2097152 | tf_op jit(solution)/shard_map/all_to_all | solution.py:140
  41.3 0.1 broadcast_multiply_fusion.2
  41.5 0.0 copy-done.2
  41.5 0.1 broadcast_and_fusion
  41.6 0.1 broadcast_add_fusion
  41.6 1.1 divide_select_fusion
  42.8 22.7 %all-to-all-done = f32[2,16,64,128]{3,1,0,2:T(8,128)S(1)} async-done(((f32[2,16,64,128]{3,1,0,2:T(8,128)}), f32[2,16,64,128]{3,1,0,2:T(8,128)S(1)}, u32[]{:S(2)}, u32[]{:S(2)}) %all-to-all-start) | async-done | bytes 1048608 | tf_op jit(solution)/shard_map/all_to_all | solution.py:140
  65.4 0.1 copy.37
  65.5 0.4 fusion.94
  66.0 0.0 copy-start.1
  66.0 0.3 maximum_bitcast_fusion.1
  66.3 0.7 copy-done.1
  67.0 1.3 %broadcast_multiply_fusion = (f32[2,64,16,128]{3,1,2,0:T(8,128)S(1)}, f32[2,16,128,64,1]{2,3,4,1,0:T(8,128)S(1)}) fusion(f32[64,16,128]{2,0,1:T(8,128)S(1)} %copy-done.1, f32[1,64,64]{2,1,0:T(8,128)S(1)} %get-tuple-element.26, f32[1,64,64]{2,1,0:T(8,128)S(1)} %get-tuple-element.27, f32[1,2,64,16,128]{4,2,0,3,1:T(8,128)S(1)} %maximum_bitcast_fusion.1, ...), kind=kOutput, calls=%fused_computation.58 | convolution fusion | flops 403447808 | bytes 4751360 | tf_op jit(solution)/shard_map/tkn,tpnbc->pkbc/dot_general | solution.py:44
  68.3 0.4 fusion.93
  68.7 0.3 maximum_bitcast_fusion.2
  69.1 1.3 %fusion.19 = f32[2,64,16,128]{3,1,0,2:T(8,128)S(1)} fusion(f32[1,64,64]{2,1,0:T(8,128)S(1)} %get-tuple-element.27, f32[1,64,64]{2,1,0:T(8,128)S(1)} %broadcast_multiply_fusion.2, f32[1,2,64,16,128]{4,2,3,1,0:T(8,128)S(1)} %maximum_bitcast_fusion.2, f32[1,2,64,16,128]{4,2,3,1,0:T(8,128)S(1)} %bitcast.151), kind=kOutput, calls=%fused_computation.30 | convolution fusion | flops 403185664 | bytes 3178496 | tf_op jit(solution)/shard_map/tkn,tpnbc->pkbc/dot_general | solution.py:44
  70.4 1.6 %copy.38 = f32[2,64,16,128]{3,2,0,1:T(8,128)} copy(f32[2,64,16,128]{3,1,0,2:T(8,128)S(1)} %fusion.19) | data formatting | bytes 2097152 | tf_op jit(solution)/shard_map/tkn,tpnbc->pkbc/transpose | solution.py:44
  72.0 3.5 %all-to-all-start.1 = ((f32[2,64,16,128]{3,2,0,1:T(8,128)}), f32[2,64,16,128]{3,2,0,1:T(8,128)S(1)}, u32[]{:S(2)}, u32[]{:S(2)}) async-start(f32[2,64,16,128]{3,2,0,1:T(8,128)} %copy.38), calls=%async_computation.1 | async-start | bytes 2097152 | tf_op jit(solution)/shard_map/all_to_all | solution.py:119
  75.5 0.1 broadcast_multiply_fusion.1
  75.7 0.4 slice_bitcast_fusion.2
  76.1 0.3 maximum_negate_fusion
  76.4 0.2 pad_maximum_fusion.3
  76.7 26.4 %fusion.28 = f32[2,2,2]{1,2,0:T(2,128)S(1)} fusion(f32[2,2,64,16,128]{4,2,3,1,0:T(8,128)S(1)} %pad_maximum_fusion.3, f32[2,64,16,128]{3,1,2,0:T(8,128)S(1)} %get-tuple-element.20), kind=kOutput, calls=%fused_computation.34 | convolution fusion | flops 12582920 | bytes 3145760 | tf_op jit(solution)/shard_map/pn,tqn->tpq/dot_general | solution.py:129
  103.1 12.2 %psum.7 = f32[2,2,2]{1,2,0:T(2,128)S(1)} all-reduce(f32[2,2,2]{1,2,0:T(2,128)S(1)} %fusion.28), channel_id=1, replica_groups=mesh['blk'=8,'space'=4] {'space'}, use_global_device_ids=true, to_apply=%region_0.1 | all-reduce | flops 8 | bytes 64 | tf_op jit(solution)/shard_map/psum | solution.py:144
  115.2 0.1 copy.44
  115.3 0.6 gather_fusion.1
  115.9 0.1 select_bitcast_fusion
  116.0 0.1 copy.45
  116.1 0.6 gather_fusion.2
  116.7 0.1 copy.46
  116.8 0.6 bitcast_select_fusion.1
  117.3 0.0 all-to-all-done.1
  117.3 0.1 copy.40
  117.5 0.4 fusion.92
  117.9 0.3 maximum_bitcast_fusion.3
  118.2 1.3 %fusion.8 = f32[2,16,128,64,1]{2,3,0,1,4:T(8,128)S(1)} fusion(f32[1,64,64]{2,1,0:T(8,128)S(1)} %get-tuple-element.27, f32[1,64,64]{2,1,0:T(8,128)S(1)} %broadcast_multiply_fusion.2, f32[1,2,16,64,128]{4,3,2,1,0:T(8,128)S(1)} %maximum_bitcast_fusion.3, f32[1,2,16,64,128]{4,3,2,1,0:T(8,128)S(1)} %bitcast.150), kind=kOutput, calls=%fused_computation.21 | convolution fusion | flops 403185664 | bytes 3178496 | tf_op jit(solution)/shard_map/tkn,tpanc->pakc/dot_general | solution.py:51
  119.5 1.0 convolution_multiply_fusion
  120.6 0.6 gather_fusion
  121.2 1.2 bitcast_select_fusion
  (8 shorter events, 0.1 us)
Async XLA Ops:
  0.6 27.3 %collective-permute-start = (bf16[1,8,2,16,4096]{4,3,2,1,0:T(8,128)(2,1)}, bf16[1,8,2,16,4096]{4,3,2,1,0:T(8,128)(2,1)S(1)}, u32[]{:S(2)}, u32[]{:S(2)}) collective-permute-start(bf16[1,8,2,16,4096]{4,3,2,1,0:T(8,128)(2,1)} %param.4), channel_id=1, source_target_pairs={{28,0},{0,4},{4,8},{8,12},{12,16},{16,20},{20,24},{24,28},{29,1},{... | collective-permute-start | bytes 6291464 | tf_op jit(solution)/shard_map/ppermute | solution.py:18
  1.7 2.2 %copy-start = (bf16[1,8,2,16,4096]{4,3,2,1,0:T(8,128)(2,1)S(1)}, bf16[1,8,2,16,4096]{4,3,2,1,0:T(8,128)(2,1)}, u32[]{:S(2)}) copy-start(bf16[1,8,2,16,4096]{4,3,2,1,0:T(8,128)(2,1)} %param.3) | copy-start | bytes 6291460
  34.0 7.5 %copy-start.2 = (s32[1,2]{1,0:T(1,128)S(1)}, s32[1,2]{1,0:T(1,128)}, u32[]{:S(2)}) copy-start(s32[1,2]{1,0:T(1,128)} %param.5) | copy-start | bytes 28
  35.6 29.8 %all-to-all-start = ((f32[2,16,64,128]{3,1,0,2:T(8,128)}), f32[2,16,64,128]{3,1,0,2:T(8,128)S(1)}, u32[]{:S(2)}, u32[]{:S(2)}) async-start(f32[2,16,64,128]{3,1,0,2:T(8,128)} %copy.36), calls=%async_computation | async-start | bytes 2097152 | tf_op jit(solution)/shard_map/all_to_all | solution.py:140
  66.0 1.0 copy-start.1
  72.0 45.3 %all-to-all-start.1 = ((f32[2,64,16,128]{3,2,0,1:T(8,128)}), f32[2,64,16,128]{3,2,0,1:T(8,128)S(1)}, u32[]{:S(2)}, u32[]{:S(2)}) async-start(f32[2,64,16,128]{3,2,0,1:T(8,128)} %copy.38), calls=%async_computation.1 | async-start | bytes 2097152 | tf_op jit(solution)/shard_map/all_to_all | solution.py:119
where the time goes:
time: 123 us; the launch traced here: 122 us
  waiting for transfers between devices  46.2 us (38%)
  matrix products  33.8 us (27%)
  blocking collectives  12.2 us (10%)
  other arithmetic  10.2 us (8%)
  starting transfers between devices  9.69 us (8%)
  local copies, waits for them, and re-layouts  9.38 us (8%)
    dot_general x1, matrix products, pair_products(): return jnp.einsum('pn,tqn->tpq', flat_first, stacked, precision=PRECISE)  26.4 us
    ppermute x1, waiting for transfers between devices, shifted(): return lax.ppermute(block, axis, route)  23.6 us
    all_to_all x1, waiting for transfers between devices, shards(): lax.all_to_all(plane_spectra(densities), 'space', split_axis=2, concat_ax...  22.7 us
    psum x1, blocking collectives, shards(): totals = lax.psum(partial_sums, 'space')  12.2 us
    all_to_all x1, starting transfers between devices, shards(): lax.all_to_all(plane_spectra(densities), 'space', split_axis=2, concat_ax...  5.62 us
    all_to_all x1, starting transfers between devices, inverse_field(): lax.all_to_all(along_rows(weighted, -1.0), 'space', split_axis=1, concat_...  3.52 us
    unnamed x7, local copies, waits for them, and re-layouts  2.91 us
    dot_general x2, matrix products, along_rows(): return jnp.einsum('tkn,tpnbc->pkbc', tables, stacked, precision=PRECISE)  2.64 us
  transfers between devices with their start and end apart: 3, of which 2 were waited for; matrix products, arithmetic and copies ran while one was open for 28% of the time, Pallas kernels for 0%

commit v1 on v0

--- a/solution.py
+++ b/solution.py
@@ -10,6 +10,24 @@
 NZ = 64
 SCREENING = 0.01
 PRECISE = lax.Precision.HIGHEST
+
+
+def _rest_panels(x0, shard_axis="space"):
+    f_now = lax.psum(1, shard_axis)
+    back = lax.axis_index(shard_axis)
+    mat_out, block_next = (f_now, back)
+    clean = x0.shape[2] // mat_out
+    carry_in = list(x0.shape)
+    carry_in[2] = clean
+    a_next = carry_in[1]
+    carry_in[1] = a_next * mat_out
+    z_new = jnp.zeros(carry_in, x0.dtype)
+    for p in range(mat_out):
+        x_next = lax.dynamic_slice_in_dim(x0, (block_next ^ p) * clean, clean, axis=2)
+        if p:
+            x_next = lax.ppermute(x_next, shard_axis, [(w, w ^ p) for w in range(mat_out)])
+        z_new = lax.dynamic_update_slice_in_dim(z_new, x_next, (block_next ^ p) * a_next, axis=1)
+    return z_new
 
 
 def shifted(block, axis, distance):
@@ -136,9 +154,7 @@
     forward = partial(column_spectra, start_y=start_y)
     previous = fetch_previous(holes)
     densities = pair_densities(electrons, jnp.concatenate([holes, previous], axis=0))
-    spectra, weighted = forward(
-        lax.all_to_all(plane_spectra(densities), "space", split_axis=2, concat_axis=1, tiled=True)
-    )
+    spectra, weighted = forward(_rest_panels(plane_spectra(densities)))
     partial_sums = pair_products(weighted, spectra) * (factor * factor)
     potential_field = inverse_field(weighted, factor)
     totals = lax.psum(partial_sums, "space")

time: 123 us -> 119 us (0.967)
  waiting for transfers between devices: 46.2 us -> 41.8 us
  other arithmetic: 10.2 us -> 11.5 us
    all_to_all x1 -> x0, waiting for transfers between devices: 22.7 us -> none  [shards(): lax.all_to_all(plane_spectra(densities), 'space', split_axis=2, concat_ax...]
    ppermute x0 -> x3, waiting for transfers between devices: none -> 21 us  [_rest_panels(): lax.ppermute(x_next, shard_axis, [(w, w ^ p) for w in range(mat_out)])]
    all_to_all x1 -> x0, starting transfers between devices: 5.62 us -> none  [shards(): lax.all_to_all(plane_spectra(densities), 'space', split_axis=2, concat_ax...]
    ppermute x0 -> x3, starting transfers between devices: none -> 5.13 us  [_rest_panels(): lax.ppermute(x_next, shard_axis, [(w, w ^ p) for w in range(mat_out)])]
    ppermute x1, waiting for transfers between devices: 23.6 us -> 20.8 us  [shifted(): return lax.ppermute(block, axis, route)]
    transpose x1 -> x0, local copies, waits for them, and re-layouts: 1.58 us -> none  [along_columns(): return jnp.einsum('tkn,tpanc->pakc', tables, stacked, precision=PRECISE)]
    unnamed x7 -> x5, local copies, waits for them, and re-layouts: 2.91 us -> 2.91 us
  transfers between devices with their start and end apart: 3 -> 5, of which waited for: 2 -> 3; matrix products, arithmetic and copies ran while one was open for 28% -> 30% of each run, Pallas kernels for 0% -> 0%
where the time goes in v1:
time: 119 us; the launch traced here: 118 us
  waiting for transfers between devices  41.8 us (35%)
  matrix products  33.8 us (28%)
  blocking collectives  12.2 us (10%)
  other arithmetic  11.5 us (10%)
  starting transfers between devices  9.59 us (8%)
  local copies, waits for them, and re-layouts  8.39 us (7%)
    dot_general x1, matrix products, pair_products(): return jnp.einsum('pn,tqn->tpq', flat_first, stacked, precision=PRECISE)  26.4 us
    ppermute x3, waiting for transfers between devices, _rest_panels(): lax.ppermute(x_next, shard_axis, [(w, w ^ p) for w in range(mat_out)])  21 us
    ppermute x1, waiting for transfers between devices, shifted(): return lax.ppermute(block, axis, route)  20.8 us
    psum x1, blocking collectives, shards(): totals = lax.psum(partial_sums, 'space')  12.2 us
    ppermute x3, starting transfers between devices, _rest_panels(): lax.ppermute(x_next, shard_axis, [(w, w ^ p) for w in range(mat_out)])  5.13 us
    all_to_all x1, starting transfers between devices, inverse_field(): lax.all_to_all(along_rows(weighted, -1.0), 'space', split_axis=1, concat_...  3.92 us
    unnamed x5, local copies, waits for them, and re-layouts  2.91 us
    dot_general x2, matrix products, along_rows(): return jnp.einsum('tkn,tpnbc->pkbc', tables, stacked, precision=PRECISE)  2.64 us
  transfers between devices with their start and end apart: 5, of which 3 were waited for; matrix products, arithmetic and copies ran while one was open for 30% of the time, Pallas kernels for 0%

profile of v1, /device:TPU:0, one launch (start us, length us, event | category | flops | bytes accessed | tf_op | source)
XLA Modules:
  0.0 118.2 jit_solution(894829154672568665)
XLA Ops:
  0.6 0.5 collective-permute-start
  1.2 0.7 compare_and_fusion
  1.8 0.7 fusion.81
  2.6 0.1 fusion.68
  2.8 0.1 fusion.66
  2.9 0.1 fusion.64
  3.1 0.1 broadcast_and_fusion
  3.2 0.1 broadcast_add_fusion
  3.3 1.1 divide_select_fusion
  4.4 1.9 %constant_dynamic-update-slice_fusion.1 = bf16[2,8,2,16,4096]{4,3,2,1,0:T(8,128)(2,1)S(1)} fusion(bf16[1,8,2,16,4096]{4,3,2,1,0:T(8,128)(2,1)} %param.4), kind=kLoop, calls=%fused_computation.115 | loop fusion | bytes 4194304
  6.3 0.3 copy-done
  6.7 0.5 bitcast_convert_fusion.1
  7.1 20.8 %collective-permute-done = bf16[1,8,2,16,4096]{4,3,2,1,0:T(8,128)(2,1)S(1)} collective-permute-done((bf16[1,8,2,16,4096]{4,3,2,1,0:T(8,128)(2,1)}, bf16[1,8,2,16,4096]{4,3,2,1,0:T(8,128)(2,1)S(1)}, u32[]{:S(2)}, u32[]{:S(2)}) %collective-permute-start) | collective-permute-done | bytes 2097184 | tf_op jit(solution)/shard_map/ppermute | solution.py:36
  28.0 0.2 constant_dynamic-update-slice_fusion
  28.2 1.7 %fusion.2 = (f32[16,4096,2]{1,0,2:T(8,128)S(1)}, f32[16,4096,2]{1,0,2:T(8,128)S(1)}, f32[16,4096,2]{1,0,2:T(8,128)S(1)}, f32[16,4096,2]{1,0,2:T(8,128)S(1)}) fusion(f32[16,4096,8]{1,0,2:T(8,128)S(1)} %get-tuple-element.9, bf16[2,8,2,16,4096]{4,3,2,1,0:T(8,128)(2,1)S(1)} %constant_dynamic-update-slice_fusion, f32[16,4096,8]{1,0,2:T(8,128)S(1)} %get-tuple-element.8), kind=kLoop, calls=%fused_computation.9 | loop fusion | flops 9961472 | bytes 10485760 | tf_op jit(solution)/shard_map/ebxc,hbxc->hexc/dot_general | solution.py:102
  29.9 0.1 subtract_bitcast_fusion
  30.0 0.4 reshape.325
  30.4 0.4 reshape.324
  30.8 1.1 fusion.29
  31.9 0.4 fusion.92
  32.3 0.3 maximum_bitcast_fusion
  32.7 1.3 %fusion.12 = f32[2,16,128,64,1]{2,3,0,1,4:T(8,128)S(1)} fusion(f32[1,64,64]{2,1,0:T(8,128)S(1)} %get-tuple-element.31, f32[1,64,64]{2,1,0:T(8,128)S(1)} %get-tuple-element.30, f32[1,2,16,64,128]{4,3,2,1,0:T(8,128)S(1)} %maximum_bitcast_fusion, f32[1,2,16,64,128]{4,3,2,1,0:T(8,128)S(1)} %bitcast.152), kind=kOutput, calls=%fused_computation.25 | convolution fusion | flops 403185664 | bytes 3178496 | tf_op jit(solution)/shard_map/tkn,tpanc->pakc/dot_general | solution.py:69
  34.0 0.1 copy.134
  34.1 0.1 dynamic-slice_bitcast_fusion
  34.2 2.4 %collective-permute-start.1 = (f32[2,16,16,128]{3,2,1,0:T(8,128)S(1)}, f32[2,16,16,128]{3,2,1,0:T(8,128)S(1)}, u32[]{:S(2)}, u32[]{:S(2)}) collective-permute-start(f32[2,16,16,128]{3,2,1,0:T(8,128)S(1)} %get-tuple-element.20), channel_id=1, source_target_pairs={{0,1},{1,0},{2,3},{3,2},{4,5},{5,4},{6,7},{7,6},{8,9},{9,8},{10,11... | collective-permute-start | bytes 786440 | tf_op jit(solution)/shard_map/ppermute | solution.py:28
  36.6 0.1 broadcast_multiply_fusion.2
  36.7 2.5 %collective-permute-start.3 = (f32[2,16,16,128]{3,2,1,0:T(8,128)S(1)}, f32[2,16,16,128]{3,2,1,0:T(8,128)S(1)}, u32[]{:S(2)}, u32[]{:S(2)}) collective-permute-start(f32[2,16,16,128]{3,2,1,0:T(8,128)S(1)} %get-tuple-element.18), channel_id=1, source_target_pairs={{0,3},{1,2},{2,1},{3,0},{4,7},{5,6},{6,5},{7,4},{8,11},{9,10},{10,... | collective-permute-start | bytes 786440 | tf_op jit(solution)/shard_map/ppermute | solution.py:28
  39.3 0.2 collective-permute-start.2
  39.5 0.1 broadcast_in_dim.20
  39.6 0.1 copy_dynamic-update-slice_fusion.3
  39.7 3.6 %collective-permute-done.1 = f32[2,16,16,128]{3,2,1,0:T(8,128)S(1)} collective-permute-done((f32[2,16,16,128]{3,2,1,0:T(8,128)S(1)}, f32[2,16,16,128]{3,2,1,0:T(8,128)S(1)}, u32[]{:S(2)}, u32[]{:S(2)}) %collective-permute-start.1) | collective-permute-done | bytes 262176 | tf_op jit(solution)/shard_map/ppermute | solution.py:28
  43.3 0.1 copy_dynamic-update-slice_fusion.2
  43.4 17.4 %collective-permute-done.2 = f32[2,16,16,128]{3,2,1,0:T(8,128)S(1)} collective-permute-done((f32[2,16,16,128]{3,2,1,0:T(8,128)S(1)}, f32[2,16,16,128]{3,2,1,0:T(8,128)S(1)}, u32[]{:S(2)}, u32[]{:S(2)}) %collective-permute-start.2) | collective-permute-done | bytes 262176 | tf_op jit(solution)/shard_map/ppermute | solution.py:28
  60.8 0.1 copy_dynamic-update-slice_fusion.1
  60.9 0.1 copy_dynamic-update-slice_fusion
  61.0 0.4 fusion.91
  61.4 0.3 maximum_bitcast_fusion.1
  61.8 0.7 copy-done.1
  62.4 1.3 %broadcast_multiply_fusion = (f32[2,64,16,128]{3,1,2,0:T(8,128)S(1)}, f32[2,16,128,64,1]{2,3,4,1,0:T(8,128)S(1)}) fusion(f32[64,16,128]{2,0,1:T(8,128)S(1)} %copy-done.1, f32[1,64,64]{2,1,0:T(8,128)S(1)} %get-tuple-element.30, f32[1,64,64]{2,1,0:T(8,128)S(1)} %get-tuple-element.31, f32[1,2,64,16,128]{4,2,0,3,1:T(8,128)S(1)} %maximum_bitcast_fusion.1, ...), kind=kOutput, calls=%fused_computation.58 | convolution fusion | flops 403447808 | bytes 4751360 | tf_op jit(solution)/shard_map/tkn,tpnbc->pkbc/dot_general | solution.py:62
  63.8 0.4 fusion.90
  64.2 0.3 maximum_bitcast_fusion.2
  64.5 1.3 %fusion.16 = f32[2,64,16,128]{3,1,0,2:T(8,128)S(1)} fusion(f32[1,64,64]{2,1,0:T(8,128)S(1)} %get-tuple-element.31, f32[1,64,64]{2,1,0:T(8,128)S(1)} %broadcast_multiply_fusion.2, f32[1,2,64,16,128]{4,2,3,1,0:T(8,128)S(1)} %maximum_bitcast_fusion.2, f32[1,2,64,16,128]{4,2,3,1,0:T(8,128)S(1)} %bitcast.155), kind=kOutput, calls=%fused_computation.29 | convolution fusion | flops 403185664 | bytes 3178496 | tf_op jit(solution)/shard_map/tkn,tpnbc->pkbc/dot_general | solution.py:62
  65.8 1.6 %copy.50 = f32[2,64,16,128]{3,2,0,1:T(8,128)} copy(f32[2,64,16,128]{3,1,0,2:T(8,128)S(1)} %fusion.16) | data formatting | bytes 2097152 | tf_op jit(solution)/shard_map/tkn,tpnbc->pkbc/transpose | solution.py:62
  67.4 3.9 %all-to-all-start = ((f32[2,64,16,128]{3,2,0,1:T(8,128)}), f32[2,64,16,128]{3,2,0,1:T(8,128)S(1)}, u32[]{:S(2)}, u32[]{:S(2)}) async-start(f32[2,64,16,128]{3,2,0,1:T(8,128)} %copy.50), calls=%async_computation | async-start | bytes 2097152 | tf_op jit(solution)/shard_map/all_to_all | solution.py:137
  71.3 0.1 broadcast_multiply_fusion.1
  71.5 0.4 slice_bitcast_fusion.2
  71.9 0.3 maximum_negate_fusion
  72.2 0.2 pad_maximum_fusion.3
  72.5 26.4 %fusion.25 = f32[2,2,2]{1,2,0:T(2,128)S(1)} fusion(f32[2,2,64,16,128]{4,2,3,1,0:T(8,128)S(1)} %pad_maximum_fusion.3, f32[2,64,16,128]{3,1,2,0:T(8,128)S(1)} %get-tuple-element.24), kind=kOutput, calls=%fused_computation.33 | convolution fusion | flops 12582920 | bytes 3145760 | tf_op jit(solution)/shard_map/pn,tqn->tpq/dot_general | solution.py:147
  98.9 12.2 %psum.7 = f32[2,2,2]{1,2,0:T(2,128)S(1)} all-reduce(f32[2,2,2]{1,2,0:T(2,128)S(1)} %fusion.25), channel_id=1, replica_groups=mesh['blk'=8,'space'=4] {'space'}, use_global_device_ids=true, to_apply=%region_0.1 | all-reduce | flops 8 | bytes 64 | tf_op jit(solution)/shard_map/psum | solution.py:160
  111.1 0.1 copy.56
  111.2 0.6 gather_fusion.1
  111.8 0.1 select_bitcast_fusion
  111.8 0.1 copy.57
  111.9 0.6 gather_fusion.2
  112.5 0.1 copy.58
  112.6 0.6 bitcast_select_fusion.1
  113.2 0.1 copy.52
  113.3 0.4 fusion.89
  113.7 0.3 maximum_bitcast_fusion.3
  114.1 1.3 %fusion.8 = f32[2,16,128,64,1]{2,3,0,1,4:T(8,128)S(1)} fusion(f32[1,64,64]{2,1,0:T(8,128)S(1)} %get-tuple-element.31, f32[1,64,64]{2,1,0:T(8,128)S(1)} %broadcast_multiply_fusion.2, f32[1,2,16,64,128]{4,3,2,1,0:T(8,128)S(1)} %maximum_bitcast_fusion.3, f32[1,2,16,64,128]{4,3,2,1,0:T(8,128)S(1)} %bitcast.154), kind=kOutput, calls=%fused_computation.21 | convolution fusion | flops 403185664 | bytes 3178496 | tf_op jit(solution)/shard_map/tkn,tpanc->pakc/dot_general | solution.py:69
  115.4 1.0 convolution_multiply_fusion
  116.5 0.6 gather_fusion
  117.1 1.2 bitcast_select_fusion
  (11 shorter events, 0.2 us)
Async XLA Ops:
  0.6 27.3 %collective-permute-start = (bf16[1,8,2,16,4096]{4,3,2,1,0:T(8,128)(2,1)}, bf16[1,8,2,16,4096]{4,3,2,1,0:T(8,128)(2,1)S(1)}, u32[]{:S(2)}, u32[]{:S(2)}) collective-permute-start(bf16[1,8,2,16,4096]{4,3,2,1,0:T(8,128)(2,1)} %param.4), channel_id=1, source_target_pairs={{28,0},{0,4},{4,8},{8,12},{12,16},{16,20},{20,24},{24,28},{29,1},{... | collective-permute-start | bytes 6291464 | tf_op jit(solution)/shard_map/ppermute | solution.py:36
  4.4 2.2 %copy-start = (bf16[1,8,2,16,4096]{4,3,2,1,0:T(8,128)(2,1)S(1)}, bf16[1,8,2,16,4096]{4,3,2,1,0:T(8,128)(2,1)}, u32[]{:S(2)}) copy-start(bf16[1,8,2,16,4096]{4,3,2,1,0:T(8,128)(2,1)} %param.3) | copy-start | bytes 6291460
  34.2 9.1 %collective-permute-start.1 = (f32[2,16,16,128]{3,2,1,0:T(8,128)S(1)}, f32[2,16,16,128]{3,2,1,0:T(8,128)S(1)}, u32[]{:S(2)}, u32[]{:S(2)}) collective-permute-start(f32[2,16,16,128]{3,2,1,0:T(8,128)S(1)} %get-tuple-element.20), channel_id=1, source_target_pairs={{0,1},{1,0},{2,3},{3,2},{4,5},{5,4},{6,7},{7,6},{8,9},{9,8},{10,11... | collective-permute-start | bytes 786440 | tf_op jit(solution)/shard_map/ppermute | solution.py:28
  36.7 24.1 %collective-permute-start.3 = (f32[2,16,16,128]{3,2,1,0:T(8,128)S(1)}, f32[2,16,16,128]{3,2,1,0:T(8,128)S(1)}, u32[]{:S(2)}, u32[]{:S(2)}) collective-permute-start(f32[2,16,16,128]{3,2,1,0:T(8,128)S(1)} %get-tuple-element.18), channel_id=1, source_target_pairs={{0,3},{1,2},{2,1},{3,0},{4,7},{5,6},{6,5},{7,4},{8,11},{9,10},{10,... | collective-permute-start | bytes 786440 | tf_op jit(solution)/shard_map/ppermute | solution.py:28
  39.3 21.5 %collective-permute-start.2 = (f32[2,16,16,128]{3,2,1,0:T(8,128)S(1)}, f32[2,16,16,128]{3,2,1,0:T(8,128)S(1)}, u32[]{:S(2)}, u32[]{:S(2)}) collective-permute-start(f32[2,16,16,128]{3,2,1,0:T(8,128)S(1)} %get-tuple-element.19), channel_id=1, source_target_pairs={{0,2},{1,3},{2,0},{3,1},{4,6},{5,7},{6,4},{7,5},{8,10},{9,11},{10,... | collective-permute-start | bytes 786440 | tf_op jit(solution)/shard_map/ppermute | solution.py:28
  61.4 1.0 copy-start.1
  67.4 45.8 %all-to-all-start = ((f32[2,64,16,128]{3,2,0,1:T(8,128)}), f32[2,64,16,128]{3,2,0,1:T(8,128)S(1)}, u32[]{:S(2)}, u32[]{:S(2)}) async-start(f32[2,64,16,128]{3,2,0,1:T(8,128)} %copy.50), calls=%async_computation | async-start | bytes 2097152 | tf_op jit(solution)/shard_map/all_to_all | solution.py:137
